TPU v7x, 32 devices: a whole 2x2x4 slice. The times are simulated.
32 devices in a mesh: seq: 2 (over core), pipe: 4 (over y, x), tp: 4 (over z).
Axes of the slice: x: 2, y: 2, z: 4, core: 2. Of those that a mesh axis runs over, the one named last changes fastest.
Arguments:
- queries: bfloat16 [4, 1024, 3072], P('pipe', 'seq', 'tp'), may hold values from -6 to 6
- keys: bfloat16 [4, 1024, 3072], P('pipe', 'seq', 'tp'), may hold values from -6 to 6
- values: bfloat16 [4, 1024, 3072], P('pipe', 'seq', 'tp'), may hold values from -6 to 6
- grad_out: bfloat16 [4, 1024, 3072], P('pipe', 'seq', 'tp'), may hold values from -6 to 6
- router: float32 [4, 1024], P('pipe', 'seq'), may hold values from 0.1 to 1
- blocks: int32 [4, 2, 3], P('pipe', 'seq'), may hold values from 0 to 3, as said below
- counts: int32 [4, 2], P('pipe', 'seq'), may hold values from 1 to 3, as said below
Outputs:
- section_grads: bfloat16 [4, 3, 768, 3072], P('pipe', None, 'seq', 'tp')
- router_grad: float32 [4, 768], P('pipe', 'seq')
Inputs may be any that keep to these rules, and one draw needn't show every extreme that they name: Per section and shard, the first counts entries are distinct block numbers in increasing order; the remaining entries are 0. In every draw some shard routes its last 3 blocks. `counts`: in every draw some shard routes 3 blocks and some routes 1.
All inputs are finite; a program needn't handle non-finite values.
Results may differ from a plain program's by a relative error of at most 0.0058.
Values may be sent and summed in bfloat16 or wider, within the bound.
No kernel may reach another device: no remote copies, remote signals or barrier semaphores. Data moves between devices by JAX's collectives and lax.ppermute only.
A program may use at most 128 MiB of HBM per device.

v0:
```python
import math
import jax
import jax.numpy as jnp
from jax import lax
from jax.sharding import PartitionSpec as P

HEAD_SIZE = 128
BLOCK_ROWS = 128


def carried_in(part, axis, combine, identity, reverse):
    count = lax.axis_size(axis)
    place = lax.axis_index(axis)
    ahead = count - 1 - place if reverse else place
    gathered = lax.all_gather(part, axis)
    state = jnp.zeros_like(part) + jnp.asarray(identity, part.dtype)

    def one(turn, state):
        source = count - 1 - turn if reverse else turn
        return combine(state, lax.dynamic_index_in_dim(gathered, source, 0, False))

    return lax.fori_loop(0, ahead, one, state)


def from_behind(x, axis, by):
    count = lax.axis_size(axis)
    return lax.ppermute(x, axis, [(i, (i + by) % count) for i in range(count)])


def plus_state(earlier, later):
    return earlier + later


def on_device(queries, keys, values, grad_out, router, blocks, counts):
    heads_dev = queries.shape[2] // HEAD_SIZE
    width_dev = queries.shape[2]
    slot_count = blocks.shape[2]
    shard_blocks = queries.shape[1] // BLOCK_ROWS
    seq_count = lax.axis_size("seq")
    factor = 1.0 / math.sqrt(HEAD_SIZE * slot_count * BLOCK_ROWS * seq_count)
    valid_slot = jnp.arange(slot_count, dtype=jnp.int32) < counts[0, 0]
    picker = (
        blocks[0, 0, :, None] == jnp.arange(shard_blocks, dtype=jnp.int32)[None, :]
    ) & valid_slot[:, None]
    picker_half = picker.astype(jnp.bfloat16)
    picker_full = picker.astype(jnp.float32)

    def select(array):
        grouped = array[0].reshape(shard_blocks, BLOCK_ROWS, width_dev)
        taken_blocks = jnp.einsum(
            "jb,btf->jtf", picker_half, grouped, preferred_element_type=jnp.float32
        ).astype(jnp.bfloat16)
        return taken_blocks.reshape(slot_count, BLOCK_ROWS, heads_dev, HEAD_SIZE)

    query_rows = select(queries)
    key_rows = select(keys)
    value_rows = select(values)
    grad_rows = select(grad_out)
    grad_wide = grad_rows.astype(jnp.float32)
    router_weight = jnp.einsum(
        "jb,bt->jt",
        picker_full,
        router[0].reshape(shard_blocks, BLOCK_ROWS),
        precision=lax.Precision.HIGHEST,
    )
    output_gradient = (router_weight.reshape(slot_count, BLOCK_ROWS, 1, 1) * grad_wide).astype(
        jnp.bfloat16
    )
    key_value = jnp.einsum(
        "nthd,nthe->nhde", key_rows, value_rows, preferred_element_type=jnp.float32
    )
    query_grad = jnp.einsum(
        "nthd,nthe->nhde", query_rows, output_gradient, preferred_element_type=jnp.float32
    )
    zero_state = jnp.zeros((1,) + key_value.shape[1:], jnp.float32)
    local_before = jnp.concatenate([zero_state, jnp.cumsum(key_value, axis=0)[:-1]], axis=0)
    flipped = jnp.flip(query_grad, axis=0)
    local_after = jnp.flip(
        jnp.concatenate([zero_state, jnp.cumsum(flipped, axis=0)[:-1]], axis=0), axis=0
    )
    shard_state = jnp.sum(key_value, axis=0)
    shard_grad = jnp.sum(query_grad, axis=0)
    empty_state = jnp.zeros_like(shard_state)
    earlier_state = carried_in(shard_state, "seq", plus_state, empty_state, False)
    later_grad = carried_in(shard_grad, "seq", plus_state, empty_state, True)
    before = (earlier_state[None] + local_before).astype(jnp.bfloat16)
    after = (later_grad[None] + local_after).astype(jnp.bfloat16)
    causal = jnp.arange(BLOCK_ROWS)[:, None] >= jnp.arange(BLOCK_ROWS)[None, :]
    grad_scores = jnp.where(
        causal,
        jnp.einsum(
            "nthe,nshe->nhts", output_gradient, value_rows, preferred_element_type=jnp.float32
        ),
        0.0,
    ).astype(jnp.bfloat16)
    scores = jnp.where(
        causal,
        jnp.einsum("nthd,nshd->nhts", query_rows, key_rows, preferred_element_type=jnp.float32),
        0.0,
    ).astype(jnp.bfloat16)
    output_core = factor * (
        jnp.einsum("nhts,nshe->nthe", scores, value_rows, preferred_element_type=jnp.float32)
        + jnp.einsum("nthd,nhde->nthe", query_rows, before, preferred_element_type=jnp.float32)
    )
    partial_router = jnp.sum(grad_wide * output_core, axis=(2, 3)).reshape(-1)
    router_grad = lax.psum(partial_router, "tp")
    query_gradient = factor * (
        jnp.einsum("nhts,nshd->nthd", grad_scores, key_rows, preferred_element_type=jnp.float32)
        + jnp.einsum("nthe,nhde->nthd", output_gradient, before, preferred_element_type=jnp.float32)
    )
    key_gradient = factor * (
        jnp.einsum("nhts,nthd->nshd", grad_scores, query_rows, preferred_element_type=jnp.float32)
        + jnp.einsum("nshe,nhde->nshd", value_rows, after, preferred_element_type=jnp.float32)
    )
    value_gradient = factor * (
        jnp.einsum("nhts,nthe->nshe", scores, output_gradient, preferred_element_type=jnp.float32)
        + jnp.einsum("nshd,nhde->nshe", key_rows, after, preferred_element_type=jnp.float32)
    )
    stacked_gradients = (
        jnp.stack([query_gradient, key_gradient, value_gradient])
        .reshape(1, 3, slot_count * BLOCK_ROWS, heads_dev * HEAD_SIZE)
        .astype(jnp.bfloat16)
    )
    handed = from_behind(stacked_gradients, "pipe", -1)
    return (handed, router_grad.reshape(1, slot_count * BLOCK_ROWS))


def solution(mesh):
    return jax.shard_map(
        on_device,
        mesh=mesh,
        in_specs=(
            P("pipe", "seq", "tp"),
            P("pipe", "seq", "tp"),
            P("pipe", "seq", "tp"),
            P("pipe", "seq", "tp"),
            P("pipe", "seq"),
            P("pipe", "seq", None),
            P("pipe", "seq"),
        ),
        out_specs=(P("pipe", None, "seq", "tp"), P("pipe", "seq")),
        check_vma=False,
    )
```

profile of v0, /device:TPU:0, one launch (start us, length us, event | category | flops | bytes accessed | tf_op | source)
XLA Modules:
  0.0 111.4 jit_solution(18025959512974319276)
XLA Ops:
  2.8 1.5 %copy.58 = f32[3,128,768]{1,2,0:T(8,128)} copy(f32[3,128,768]{2,0,1:T(4,128)S(1)} %fusion.6) | data formatting | bytes 2359296 | tf_op jit(solution)/shard_map/convert_element_type | solution.py:59
  4.4 1.8 %convolution_convert_fusion = bf16[3,128,768]{2,0,1:T(4,128)(2,1)S(1)} fusion(bf16[4,128,768]{2,1,0:T(8,128)(2,1)} %bitcast.94, pred[3,4]{1,0:T(4,128)(4,1)S(1)} %fusion.20), kind=kOutput, calls=%fused_computation.12 | convolution fusion | flops 2654208 | bytes 1376268 | tf_op jit(solution)/shard_map/jb,btf->jtf/dot_general | solution.py:50
  6.9 1.8 %convolution_convert_fusion.3 = bf16[3,128,768]{2,0,1:T(4,128)(2,1)S(1)} fusion(bf16[4,128,768]{2,1,0:T(8,128)(2,1)} %bitcast.95, pred[3,4]{1,0:T(4,128)(4,1)S(1)} %fusion.20), kind=kOutput, calls=%fused_computation.19 | convolution fusion | flops 2654208 | bytes 1376268 | tf_op jit(solution)/shard_map/jb,btf->jtf/dot_general | solution.py:50
  9.4 2.7 %convolution_convert_fusion.1 = bf16[3,128,768]{2,0,1:T(4,128)(2,1)} fusion(bf16[4,128,768]{2,1,0:T(8,128)(2,1)} %bitcast.96, pred[3,4]{1,0:T(4,128)(4,1)S(1)} %fusion.20), kind=kOutput, calls=%fused_computation.16 | convolution fusion | flops 2654208 | bytes 1376268 | tf_op jit(solution)/shard_map/jb,btf->jtf/dot_general | solution.py:50
  12.1 1.5 %copy.60 = bf16[3,128,768]{1,2,0:T(8,128)(2,1)S(1)} copy(bf16[3,128,768]{2,0,1:T(4,128)(2,1)} %convolution_convert_fusion.1) | data formatting | bytes 1179648 | tf_op jit(solution)/shard_map/convert_element_type | solution.py:52
  13.6 1.4 %multiply_convert_fusion = bf16[3,128,6,128]{1,3,2,0:T(8,128)(2,1)S(1)} fusion(f32[3,128,6,128]{1,3,2,0:T(8,128)} %bitcast.87, f32[3,128]{1,0:T(4,128)S(1)} %fusion.31), kind=kLoop, calls=%fused_computation.31 | loop fusion | flops 589824 | bytes 1771008 | tf_op jit(solution)/shard_map/convert_element_type | solution.py:66
  15.0 1.6 %fusion.27 = (f32[6,128,128]{2,1,0:T(8,128)S(1)}, f32[3,6,128,128]{3,2,1,0:T(8,128)}) fusion(bf16[3,128,6,128]{1,3,2,0:T(8,128)(2,1)S(1)} %bitcast.75, bf16[3,128,6,128]{1,3,2,0:T(8,128)(2,1)S(1)} %multiply_convert_fusion), kind=kOutput, calls=%fused_computation.47 | convolution fusion | flops 75694080 | bytes 2752512 | tf_op jit(solution)/shard_map/nthd,nthe->nhde/dot_general | solution.py:72
  16.6 1.2 %fusion.10 = bf16[3,6,128,128]{3,2,1,0:T(8,128)(2,1)} fusion(bf16[3,128,6,128]{1,3,2,0:T(8,128)(2,1)S(1)} %bitcast.76, bf16[3,128,6,128]{1,3,2,0:T(8,128)(2,1)S(1)} %bitcast.83, pred[128,128]{1,0:T(8,128)(4,1)S(1)} %iota_compare_fusion), kind=kOutput, calls=%fused_computation.23 | convolution fusion | flops 76087296 | bytes 1785856 | tf_op jit(solution)/shard_map/nthd,nshd->nhts/dot_general | solution.py:98
  18.2 1.3 %fusion.33 = f32[3,6,128,128]{3,2,1,0:T(8,128)} fusion(bf16[3,128,6,128]{1,3,2,0:T(8,128)(2,1)S(1)} %bitcast.77, bf16[3,6,128,128]{3,2,1,0:T(8,128)(2,1)S(1)} %fusion.7), kind=kOutput, calls=%fused_computation.53 | convolution fusion | flops 75497472 | bytes 2359296 | tf_op jit(solution)/shard_map/nhts,nthd->nshd/dot_general | solution.py:112
  19.5 1.5 %fusion.32 = f32[3,6,128,128]{3,2,1,0:T(8,128)} fusion(bf16[3,128,6,128]{1,3,2,0:T(8,128)(2,1)S(1)} %bitcast.84, bf16[3,6,128,128]{3,2,1,0:T(8,128)(2,1)S(1)} %fusion.7), kind=kOutput, calls=%fused_computation.52 | convolution fusion | flops 75497472 | bytes 2359296 | tf_op jit(solution)/shard_map/nhts,nshd->nthd/dot_general | solution.py:108
  21.1 2.4 %fusion.28 = (f32[6,128,128]{2,1,0:T(8,128)}, f32[3,6,128,128]{3,2,1,0:T(8,128)}) fusion(bf16[3,128,6,128]{1,3,2,0:T(8,128)(2,1)S(1)} %bitcast.85, bf16[3,128,6,128]{1,3,2,0:T(8,128)(2,1)S(1)} %bitcast.80), kind=kOutput, calls=%fused_computation.48 | convolution fusion | flops 75694080 | bytes 2752512 | tf_op jit(solution)/shard_map/nthd,nthe->nhde/dot_general | solution.py:69
  23.4 2.4 %fusion.34 = f32[3,6,128,128]{3,2,1,0:T(8,128)} fusion(bf16[3,128,6,128]{1,3,2,0:T(8,128)(2,1)S(1)} %multiply_convert_fusion, bf16[3,6,128,128]{3,2,1,0:T(8,128)(2,1)} %fusion.10), kind=kOutput, calls=%fused_computation.54 | convolution fusion | flops 75497472 | bytes 2359296 | tf_op jit(solution)/shard_map/nhts,nthe->nshe/dot_general | solution.py:116
  25.8 2.4 %rev.7 = f32[3,6,128,128]{3,2,1,0:T(8,128)} reverse(f32[3,6,128,128]{3,2,1,0:T(8,128)} %get-tuple-element.100), dimensions={0} | reverse | bytes 2359296 | tf_op jit(solution)/shard_map/jit(_flip)/rev | solution.py:77
  28.2 1.4 %fusion.30 = f32[3,6,128,128]{3,2,1,0:T(8,128)S(1)} fusion(f32[3,6,128,128]{3,2,1,0:T(8,128)} %rev.7), kind=kOutput, calls=%fused_computation.50 | output fusion | flops 589824 | bytes 2359296 | tf_op jit(solution)/shard_map/jit(cumsum)/reduce_window_sum | solution.py:79
  30.6 2.6 %all-gather.1 = f32[12,128,128]{2,1,0:T(8,128)} all-gather(f32[6,128,128]{2,1,0:T(8,128)S(1)} %get-tuple-element.99), channel_id=3, replica_groups=mesh['seq'=2,'pipe'=4,'tp'=4] {'seq'}, dimensions={0}, use_global_device_ids=true | all-gather | bytes 1179648 | tf_op jit(solution)/shard_map/all_gather | solution.py:15
  34.3 1.2 %concatenate.16 = f32[3,6,128,128]{3,2,1,0:T(8,128)S(1)} pad(f32[2,6,128,128]{3,2,1,0:T(8,128)} %slice.9, f32[]{:T(128)} %constant.41.clone.1), padding=1_0x0_0x0_0x0_0 | pad | bytes 1966084 | tf_op jit(solution)/shard_map/concatenate | solution.py:79
  37.1 1.2 %fusion.13 = bf16[3,128,6,128]{1,3,2,0:T(8,128)(2,1)} fusion(f32[3,6,128,128]{3,2,1,0:T(8,128)S(1)} %copy-done.6, bf16[3,6,128,128]{3,2,1,0:T(8,128)(2,1)S(1)} %add_convert_fusion, bf16[3,128,6,128]{1,3,2,0:T(8,128)(2,1)S(1)} %bitcast.86), kind=kOutput, calls=%fused_computation.26 | convolution fusion | flops 76382208 | bytes 2949120 | tf_op jit(solution)/shard_map/nshd,nhde->nshe/dot_general | solution.py:117
  38.3 2.4 %copy.75 = bf16[3,128,6,128]{3,2,1,0:T(8,128)(2,1)} copy(bf16[3,128,6,128]{1,3,2,0:T(8,128)(2,1)} %fusion.13) | data formatting | bytes 1179648 | tf_op jit(solution)/shard_map/mul | solution.py:115
  40.7 2.5 %stack.14 = bf16[1,1,384,768]{3,2,1,0:T(8,128)(2,1)} reshape(bf16[3,128,6,128]{3,2,1,0:T(8,128)(2,1)} %copy.75) | data formatting | bytes 1179648 | tf_op jit(solution)/shard_map/stack | solution.py:120
  43.1 2.4 %fusion.14 = bf16[3,128,6,128]{1,3,2,0:T(8,128)(2,1)} fusion(f32[3,6,128,128]{3,2,1,0:T(8,128)} %fusion.33, bf16[3,6,128,128]{3,2,1,0:T(8,128)(2,1)S(1)} %copy-done.5, bf16[3,128,6,128]{1,3,2,0:T(8,128)(2,1)S(1)} %bitcast.81), kind=kOutput, calls=%fused_computation.27 | convolution fusion | flops 76382208 | bytes 2949120 | tf_op jit(solution)/shard_map/nshe,nhde->nshd/dot_general | solution.py:113
  45.5 2.3 %copy.70 = bf16[3,128,6,128]{3,2,1,0:T(8,128)(2,1)} copy(bf16[3,128,6,128]{1,3,2,0:T(8,128)(2,1)} %fusion.14) | data formatting | bytes 1179648 | tf_op jit(solution)/shard_map/mul | solution.py:111
  47.8 2.5 %stack.13 = bf16[1,1,384,768]{3,2,1,0:T(8,128)(2,1)} reshape(bf16[3,128,6,128]{3,2,1,0:T(8,128)(2,1)} %copy.70) | data formatting | bytes 1179648 | tf_op jit(solution)/shard_map/stack | solution.py:120
  50.3 1.4 %fusion.29 = f32[3,6,128,128]{3,2,1,0:T(8,128)S(1)} fusion(f32[3,6,128,128]{3,2,1,0:T(8,128)} %get-tuple-element.102), kind=kOutput, calls=%fused_computation.49 | output fusion | flops 589824 | bytes 2359296 | tf_op jit(solution)/shard_map/jit(cumsum)/reduce_window_sum | solution.py:76
  52.7 2.5 %all-gather = f32[12,128,128]{2,1,0:T(8,128)} all-gather(f32[6,128,128]{2,1,0:T(8,128)S(1)} %copy-done.7), channel_id=2, replica_groups=mesh['seq'=2,'pipe'=4,'tp'=4] {'seq'}, dimensions={0}, use_global_device_ids=true | all-gather | bytes 1179648 | tf_op jit(solution)/shard_map/all_gather | solution.py:15
  55.5 2.6 %fusion.15 = bf16[3,128,6,128]{1,3,2,0:T(8,128)(2,1)} fusion(f32[3,6,128,128]{3,2,1,0:T(8,128)} %fusion.32, bf16[3,128,6,128]{1,3,2,0:T(8,128)(2,1)S(1)} %multiply_convert_fusion, f32[2,6,128,128]{3,2,1,0:T(8,128)} %slice.8, f32[6,128,128]{2,1,0:T(8,128)S(1)} %get-tuple-element.81), kind=kOutput, calls=%fused_computation.28 | convolution fusion | flops 76972032 | bytes 3538944 | tf_op jit(solution)/shard_map/nthe,nhde->nthd/dot_general | solution.py:109
  58.1 2.3 %copy.65 = bf16[3,128,6,128]{3,2,1,0:T(8,128)(2,1)} copy(bf16[3,128,6,128]{1,3,2,0:T(8,128)(2,1)} %fusion.15) | data formatting | bytes 1179648 | tf_op jit(solution)/shard_map/mul | solution.py:107
  60.4 2.5 %stack.12 = bf16[1,1,384,768]{3,2,1,0:T(8,128)(2,1)} reshape(bf16[3,128,6,128]{3,2,1,0:T(8,128)(2,1)} %copy.65) | data formatting | bytes 1179648 | tf_op jit(solution)/shard_map/stack | solution.py:120
  62.9 2.9 %pad_maximum_fusion = bf16[1,3,384,768]{3,2,1,0:T(8,128)(2,1)} fusion(bf16[1,1,384,768]{3,2,1,0:T(8,128)(2,1)} %stack.14, bf16[1,1,384,768]{3,2,1,0:T(8,128)(2,1)} %stack.13, bf16[1,1,384,768]{3,2,1,0:T(8,128)(2,1)} %stack.12), kind=kLoop, calls=%fused_computation.2 | loop fusion | flops 1769472 | bytes 3538944 | tf_op jit(solution)/shard_map/stack | solution.py:120
  65.7 3.8 %collective-permute-start = (bf16[1,3,384,768]{3,2,1,0:T(8,128)(2,1)}, bf16[1,3,384,768]{3,2,1,0:T(8,128)(2,1)}, u32[]{:S(2)}, u32[]{:S(2)}) collective-permute-start(bf16[1,3,384,768]{3,2,1,0:T(8,128)(2,1)} %pad_maximum_fusion), channel_id=1, source_target_pairs={{0,12},{4,0},{8,4},{12,8},{1,13},{5,1},{9,5},{13,9},{2,14},{6,2},{... | collective-permute-start | bytes 5308424 | tf_op jit(solution)/shard_map/ppermute | solution.py:27
  70.6 12.6 %psum.7 = f32[1,384]{1,0:T(1,128)} all-reduce(f32[1,384]{1,0:T(1,128)S(1)} %bitcast.92), channel_id=1, replica_groups=mesh['seq'=2,'pipe'=4,'tp'=4] {'tp'}, use_global_device_ids=true, to_apply=%region_9.10 | all-reduce | flops 384 | bytes 3072 | tf_op jit(solution)/shard_map/psum | solution.py:106
  83.2 25.4 %collective-permute-done = bf16[1,3,384,768]{3,2,1,0:T(8,128)(2,1)} collective-permute-done((bf16[1,3,384,768]{3,2,1,0:T(8,128)(2,1)}, bf16[1,3,384,768]{3,2,1,0:T(8,128)(2,1)}, u32[]{:S(2)}, u32[]{:S(2)}) %collective-permute-start) | collective-permute-done | bytes 1769504 | tf_op jit(solution)/shard_map/ppermute | solution.py:27
  108.6 2.8 %copy.116 = bf16[1,3,384,768]{3,2,1,0:T(8,128)(2,1)} copy(bf16[1,3,384,768]{3,2,1,0:T(8,128)(2,1)} %collective-permute-done) | data formatting | bytes 3538944
  (37 shorter events, 10.2 us)
Async XLA Ops:
  0.6 1.5 %copy-start = (bf16[1,512,768]{2,1,0:T(8,128)(2,1)S(1)}, bf16[1,512,768]{2,1,0:T(8,128)(2,1)}, u32[]{:S(2)}) copy-start(bf16[1,512,768]{2,1,0:T(8,128)(2,1)} %param.14) | copy-start | bytes 2359300
  2.8 1.5 %copy-start.8 = (f32[1,512]{1,0:T(1,128)S(1)}, f32[1,512]{1,0:T(1,128)}, u32[]{:S(2)}) copy-start(f32[1,512]{1,0:T(1,128)} %param.15) | copy-start | bytes 6148
  35.6 1.5 %copy-start.6 = (f32[3,6,128,128]{3,2,1,0:T(8,128)S(1)}, f32[3,6,128,128]{3,2,1,0:T(8,128)}, u32[]{:S(2)}) copy-start(f32[3,6,128,128]{3,2,1,0:T(8,128)} %fusion.34) | copy-start | bytes 3538948
  35.7 0.8 copy-start.4
  38.3 4.8 %copy-start.5 = (bf16[3,6,128,128]{3,2,1,0:T(8,128)(2,1)S(1)}, bf16[3,6,128,128]{3,2,1,0:T(8,128)(2,1)}, u32[]{:S(2)}) copy-start(bf16[3,6,128,128]{3,2,1,0:T(8,128)(2,1)} %copy-done.4) | copy-start | bytes 1769476
  51.7 1.1 copy-start.7
  62.9 6.7 %copy-start.3 = (bf16[3,6,128,128]{3,2,1,0:T(8,128)(2,1)S(1)}, bf16[3,6,128,128]{3,2,1,0:T(8,128)(2,1)}, u32[]{:S(2)}) copy-start(bf16[3,6,128,128]{3,2,1,0:T(8,128)(2,1)} %fusion.10) | copy-start | bytes 1769476
  65.7 4.4 %copy-start.1 = (f32[3,128,768]{1,2,0:T(8,128)S(1)}, f32[3,128,768]{1,2,0:T(8,128)}, u32[]{:S(2)}) copy-start(f32[3,128,768]{1,2,0:T(8,128)} %copy.58) | copy-start | bytes 3538948
  65.7 4.4 %copy-start.2 = (f32[2,6,128,128]{3,2,1,0:T(8,128)S(1)}, f32[2,6,128,128]{3,2,1,0:T(8,128)}, u32[]{:S(2)}) copy-start(f32[2,6,128,128]{3,2,1,0:T(8,128)} %slice.8) | copy-start | bytes 2359300
  65.7 42.8 %collective-permute-start = (bf16[1,3,384,768]{3,2,1,0:T(8,128)(2,1)}, bf16[1,3,384,768]{3,2,1,0:T(8,128)(2,1)}, u32[]{:S(2)}, u32[]{:S(2)}) collective-permute-start(bf16[1,3,384,768]{3,2,1,0:T(8,128)(2,1)} %pad_maximum_fusion), channel_id=1, source_target_pairs={{0,12},{4,0},{8,4},{12,8},{1,13},{5,1},{9,5},{13,9},{2,14},{6,2},{... | collective-permute-start | bytes 5308424 | tf_op jit(solution)/shard_map/ppermute | solution.py:27
where the time goes:
time: 112 us; the launch traced here: 111 us
  local copies, waits for them, and re-layouts  28.5 us (25%)
  waiting for transfers between devices  25.4 us (23%)
  matrix products  25.3 us (23%)
  blocking collectives  17.7 us (16%)
  other arithmetic  8.97 us (8%)
  starting transfers between devices  3.82 us (3%)
  between operations  1.55 us (1%)
    ppermute x1, waiting for transfers between devices, from_behind(): return lax.ppermute(x, axis, [(i, (i + by) % count) for i in range(count)])  25.4 us
    psum x1, blocking collectives, on_device(): router_grad = lax.psum(partial_router, 'tp')  12.6 us
    another operation x3, local copies, waits for them, and re-layouts, on_device(): jnp.stack([query_gradient, key_gradient, value_gradient])  7.38 us
    dot_general x4, matrix products, select(): jnp.einsum('jb,btf->jtf', picker_half, grouped, preferred_element_type=jn...  7.09 us
    all_gather x2, blocking collectives, carried_in(): gathered = lax.all_gather(part, axis)  5.1 us
    unnamed x20, local copies, waits for them, and re-layouts  4.28 us
    ppermute x1, starting transfers between devices, from_behind(): return lax.ppermute(x, axis, [(i, (i + by) % count) for i in range(count)])  3.82 us
    another operation x1, other arithmetic, on_device(): jnp.stack([query_gradient, key_gradient, value_gradient])  2.88 us
  transfers between devices with their start and end apart: 1, of which 1 were waited for; matrix products, arithmetic and copies ran while one was open for 1% of the time, Pallas kernels for 0%

commit v1 on v0

--- a/solution.py
+++ b/solution.py
@@ -103,7 +103,11 @@
         + jnp.einsum("nthd,nhde->nthe", query_rows, before, preferred_element_type=jnp.float32)
     )
     partial_router = jnp.sum(grad_wide * output_core, axis=(2, 3)).reshape(-1)
-    router_grad = lax.psum(partial_router, "tp")
+    router_grad = partial_router
+    for hop in (1, 2):
+        router_grad = router_grad + lax.ppermute(
+            router_grad, "tp", [(dev, dev ^ hop) for dev in range(4)]
+        )
     query_gradient = factor * (
         jnp.einsum("nhts,nshd->nthd", grad_scores, key_rows, preferred_element_type=jnp.float32)
         + jnp.einsum("nthe,nhde->nthd", output_gradient, before, preferred_element_type=jnp.float32)

time: 112 us -> 104 us (0.929)
  blocking collectives: 17.7 us -> 6.2 us
  waiting for transfers between devices: 25.4 us -> 31.4 us
  starting transfers between devices: 3.82 us -> 7.86 us
  matrix products: 25.3 us -> 22.1 us
  other arithmetic: 8.97 us -> 6.27 us
    psum x1 -> x0, blocking collectives: 12.6 us -> none  [on_device(): router_grad = lax.psum(partial_router, 'tp')]
    ppermute x0 -> x2, starting transfers between devices: none -> 4.25 us  [on_device(): lax.ppermute(router_grad, 'tp', [(dev, dev ^ hop) for dev in range(4)])]
    ppermute x0 -> x2, waiting for transfers between devices: none -> 3.88 us  [on_device(): lax.ppermute(router_grad, 'tp', [(dev, dev ^ hop) for dev in range(4)])]
    ppermute x1, waiting for transfers between devices: 25.4 us -> 27.6 us  [from_behind(): return lax.ppermute(x, axis, [(i, (i + by) % count) for i in range(count)])]
    dot_general x1, matrix products: 2.39 us -> 0.31 us  [on_device(): jnp.einsum('nhts,nthe->nshe', scores, output_gradient, preferred_element_...]
    another operation x1, other arithmetic: 2.88 us -> 1.43 us  [on_device(): jnp.stack([query_gradient, key_gradient, value_gradient])]
    dot_general x1, matrix products: 2.42 us -> 1.14 us  [on_device(): jnp.einsum('nshe,nhde->nshd', value_rows, after, preferred_element_type=j...]
    convert_element_type x1, other arithmetic: 1.41 us -> 0.14 us  [on_device(): (router_weight.reshape(slot_count, BLOCK_ROWS, 1, 1) * grad_wide).astype(...]
  transfers between devices with their start and end apart: 1 -> 3, of which waited for: 1 -> 3; matrix products, arithmetic and copies ran while one was open for 1% -> 2% of each run, Pallas kernels for 0% -> 0%
where the time goes in v1:
time: 104 us; the launch traced here: 103 us
  waiting for transfers between devices  31.4 us (30%)
  local copies, waits for them, and re-layouts  27.4 us (26%)
  matrix products  22.1 us (21%)
  starting transfers between devices  7.86 us (8%)
  other arithmetic  6.27 us (6%)
  blocking collectives  6.2 us (6%)
  between operations  1.59 us (2%)
    ppermute x1, waiting for transfers between devices, from_behind(): return lax.ppermute(x, axis, [(i, (i + by) % count) for i in range(count)])  27.6 us
    another operation x3, local copies, waits for them, and re-layouts, on_device(): jnp.stack([query_gradient, key_gradient, value_gradient])  7.39 us
    dot_general x4, matrix products, select(): jnp.einsum('jb,btf->jtf', picker_half, grouped, preferred_element_type=jn...  7.32 us
    all_gather x2, blocking collectives, carried_in(): gathered = lax.all_gather(part, axis)  6.2 us
    ppermute x2, starting transfers between devices, on_device(): lax.ppermute(router_grad, 'tp', [(dev, dev ^ hop) for dev in range(4)])  4.25 us
    ppermute x2, waiting for transfers between devices, on_device(): lax.ppermute(router_grad, 'tp', [(dev, dev ^ hop) for dev in range(4)])  3.88 us
    unnamed x29, local copies, waits for them, and re-layouts  3.65 us
    ppermute x1, starting transfers between devices, from_behind(): return lax.ppermute(x, axis, [(i, (i + by) % count) for i in range(count)])  3.61 us
  transfers between devices with their start and end apart: 3, of which 3 were waited for; matrix products, arithmetic and copies ran while one was open for 2% of the time, Pallas kernels for 0%

profile of v1, /device:TPU:0, one launch (start us, length us, event | category | flops | bytes accessed | tf_op | source)
XLA Modules:
  0.0 103.1 jit_solution(5011562606722356653)
XLA Ops:
  3.5 1.8 %convolution_convert_fusion.3 = bf16[3,128,768]{2,0,1:T(4,128)(2,1)S(1)} fusion(bf16[4,128,768]{2,1,0:T(8,128)(2,1)} %bitcast.91, pred[3,4]{1,0:T(4,128)(4,1)S(1)} %fusion.20), kind=kOutput, calls=%fused_computation.19 | convolution fusion | flops 2654208 | bytes 1376268 | tf_op jit(solution)/shard_map/jb,btf->jtf/dot_general | solution.py:50
  5.9 2.9 %convolution_convert_fusion.1 = bf16[3,128,768]{2,0,1:T(4,128)(2,1)} fusion(bf16[4,128,768]{2,1,0:T(8,128)(2,1)} %bitcast.92, pred[3,4]{1,0:T(4,128)(4,1)S(1)} %fusion.20), kind=kOutput, calls=%fused_computation.16 | convolution fusion | flops 2654208 | bytes 1376268 | tf_op jit(solution)/shard_map/jb,btf->jtf/dot_general | solution.py:50
  8.9 1.5 %copy.60 = bf16[3,128,768]{1,2,0:T(8,128)(2,1)S(1)} copy(bf16[3,128,768]{2,0,1:T(4,128)(2,1)} %convolution_convert_fusion.1) | data formatting | bytes 1179648 | tf_op jit(solution)/shard_map/convert_element_type | solution.py:52
  10.4 1.8 %fusion.6 = f32[3,128,768]{2,0,1:T(4,128)} fusion(bf16[4,128,768]{2,1,0:T(8,128)(2,1)S(1)} %bitcast.88, pred[3,4]{1,0:T(4,128)(4,1)S(1)} %fusion.20), kind=kOutput, calls=%fused_computation.18 | convolution fusion | flops 2949120 | bytes 1966092 | tf_op jit(solution)/shard_map/jb,btf->jtf/dot_general | solution.py:50
  12.3 2.4 %copy.58 = f32[3,128,768]{1,2,0:T(8,128)} copy(f32[3,128,768]{2,0,1:T(4,128)} %fusion.6) | data formatting | bytes 2359296 | tf_op jit(solution)/shard_map/convert_element_type | solution.py:59
  14.8 1.6 %fusion.28 = (f32[6,128,128]{2,1,0:T(8,128)S(1)}, f32[3,6,128,128]{3,2,1,0:T(8,128)}) fusion(bf16[3,128,6,128]{1,3,2,0:T(8,128)(2,1)S(1)} %bitcast.80, bf16[3,128,6,128]{1,3,2,0:T(8,128)(2,1)S(1)} %bitcast.76), kind=kOutput, calls=%fused_computation.48 | convolution fusion | flops 75694080 | bytes 2752512 | tf_op jit(solution)/shard_map/nthd,nthe->nhde/dot_general | solution.py:69
  16.4 1.2 %fusion.10 = bf16[3,6,128,128]{3,2,1,0:T(8,128)(2,1)} fusion(bf16[3,128,6,128]{1,3,2,0:T(8,128)(2,1)S(1)} %bitcast.72, bf16[3,128,6,128]{1,3,2,0:T(8,128)(2,1)S(1)} %bitcast.81, pred[128,128]{1,0:T(8,128)(4,1)S(1)} %iota_compare_fusion), kind=kOutput, calls=%fused_computation.23 | convolution fusion | flops 76087296 | bytes 1785856 | tf_op jit(solution)/shard_map/nthd,nshd->nhts/dot_general | solution.py:98
  17.8 2.3 %fusion.27 = (f32[6,128,128]{2,1,0:T(8,128)}, f32[3,6,128,128]{3,2,1,0:T(8,128)}) fusion(bf16[3,128,6,128]{1,3,2,0:T(8,128)(2,1)S(1)} %bitcast.73, bf16[3,128,6,128]{1,3,2,0:T(8,128)(2,1)S(1)} %multiply_convert_fusion), kind=kOutput, calls=%fused_computation.47 | convolution fusion | flops 75694080 | bytes 2752512 | tf_op jit(solution)/shard_map/nthd,nthe->nhde/dot_general | solution.py:72
  20.5 1.3 %fusion.33 = f32[3,6,128,128]{3,2,1,0:T(8,128)} fusion(bf16[3,128,6,128]{1,3,2,0:T(8,128)(2,1)S(1)} %bitcast.74, bf16[3,6,128,128]{3,2,1,0:T(8,128)(2,1)S(1)} %fusion.7), kind=kOutput, calls=%fused_computation.53 | convolution fusion | flops 75497472 | bytes 2359296 | tf_op jit(solution)/shard_map/nhts,nthd->nshd/dot_general | solution.py:116
  21.9 1.5 %fusion.32 = f32[3,6,128,128]{3,2,1,0:T(8,128)} fusion(bf16[3,128,6,128]{1,3,2,0:T(8,128)(2,1)S(1)} %bitcast.82, bf16[3,6,128,128]{3,2,1,0:T(8,128)(2,1)S(1)} %fusion.7), kind=kOutput, calls=%fused_computation.52 | convolution fusion | flops 75497472 | bytes 2359296 | tf_op jit(solution)/shard_map/nhts,nshd->nthd/dot_general | solution.py:112
  23.4 2.6 %all-gather = f32[12,128,128]{2,1,0:T(8,128)} all-gather(f32[6,128,128]{2,1,0:T(8,128)S(1)} %get-tuple-element.101), channel_id=2, replica_groups=mesh['seq'=2,'pipe'=4,'tp'=4] {'seq'}, dimensions={0}, use_global_device_ids=true | all-gather | bytes 1179648 | tf_op jit(solution)/shard_map/all_gather | solution.py:15
  26.1 1.4 %fusion.29 = f32[3,6,128,128]{3,2,1,0:T(8,128)S(1)} fusion(f32[3,6,128,128]{3,2,1,0:T(8,128)} %get-tuple-element.102), kind=kOutput, calls=%fused_computation.49 | output fusion | flops 589824 | bytes 2359296 | tf_op jit(solution)/shard_map/jit(cumsum)/reduce_window_sum | solution.py:76
  28.5 3.6 %all-gather.1 = f32[12,128,128]{2,1,0:T(8,128)} all-gather(f32[6,128,128]{2,1,0:T(8,128)S(1)} %copy-done.11), channel_id=3, replica_groups=mesh['seq'=2,'pipe'=4,'tp'=4] {'seq'}, dimensions={0}, use_global_device_ids=true | all-gather | bytes 1179648 | tf_op jit(solution)/shard_map/all_gather | solution.py:15
  32.1 1.3 %while.23 = (s32[]{:T(128)}, f32[6,128,128]{2,1,0:T(8,128)S(1)}, s32[]{:T(128)}, f32[2,6,128,128]{3,2,1,0:T(8,128)}, s32[]{:T(128)}, /*index=5*/s32[]{:T(128)}, s32[]{:T(128)}) while((s32[]{:T(128)}, f32[6,128,128]{2,1,0:T(8,128)S(1)}, s32[]{:T(128)}, f32[2,6,128,128]{3,2,1,0:T(8,128)}, s32[]{:T(128)}, /*index=5*/s32[]{:T(128)}, ...), condition=%wide.region_6.7_spmd, body=%wide.region_5.6_spmd.sunk | while | flops 98310 | bytes 1179775 | solution.py:22
  33.4 2.4 %rev.7 = f32[3,6,128,128]{3,2,1,0:T(8,128)} reverse(f32[3,6,128,128]{3,2,1,0:T(8,128)} %get-tuple-element.100), dimensions={0} | reverse | bytes 2359296 | tf_op jit(solution)/shard_map/jit(_flip)/rev | solution.py:77
  35.8 1.4 %fusion.30 = f32[3,6,128,128]{3,2,1,0:T(8,128)S(1)} fusion(f32[3,6,128,128]{3,2,1,0:T(8,128)} %rev.7), kind=kOutput, calls=%fused_computation.50 | output fusion | flops 589824 | bytes 2359296 | tf_op jit(solution)/shard_map/jit(cumsum)/reduce_window_sum | solution.py:79
  40.0 2.4 %copy.70 = bf16[3,128,6,128]{3,2,1,0:T(8,128)(2,1)} copy(bf16[3,128,6,128]{1,3,2,0:T(8,128)(2,1)} %fusion.14) | data formatting | bytes 1179648 | tf_op jit(solution)/shard_map/mul | solution.py:115
  42.4 2.5 %stack.13 = bf16[1,1,384,768]{3,2,1,0:T(8,128)(2,1)} reshape(bf16[3,128,6,128]{3,2,1,0:T(8,128)(2,1)} %copy.70) | data formatting | bytes 1179648 | tf_op jit(solution)/shard_map/stack | solution.py:124
  46.1 1.2 %fusion.13 = bf16[3,128,6,128]{1,3,2,0:T(8,128)(2,1)} fusion(f32[3,6,128,128]{3,2,1,0:T(8,128)S(1)} %fusion.34, bf16[3,6,128,128]{3,2,1,0:T(8,128)(2,1)S(1)} %copy-done.8, bf16[3,128,6,128]{1,3,2,0:T(8,128)(2,1)S(1)} %bitcast.83), kind=kOutput, calls=%fused_computation.26 | convolution fusion | flops 76382208 | bytes 2949120 | tf_op jit(solution)/shard_map/nshd,nhde->nshe/dot_general | solution.py:121
  47.3 2.3 %copy.75 = bf16[3,128,6,128]{3,2,1,0:T(8,128)(2,1)} copy(bf16[3,128,6,128]{1,3,2,0:T(8,128)(2,1)} %fusion.13) | data formatting | bytes 1179648 | tf_op jit(solution)/shard_map/mul | solution.py:119
  49.6 2.5 %stack.14 = bf16[1,1,384,768]{3,2,1,0:T(8,128)(2,1)} reshape(bf16[3,128,6,128]{3,2,1,0:T(8,128)(2,1)} %copy.75) | data formatting | bytes 1179648 | tf_op jit(solution)/shard_map/stack | solution.py:124
  52.0 2.6 %fusion.15 = bf16[3,128,6,128]{1,3,2,0:T(8,128)(2,1)} fusion(f32[3,6,128,128]{3,2,1,0:T(8,128)} %fusion.32, bf16[3,128,6,128]{1,3,2,0:T(8,128)(2,1)S(1)} %multiply_convert_fusion, f32[2,6,128,128]{3,2,1,0:T(8,128)} %slice.8, f32[6,128,128]{2,1,0:T(8,128)S(1)} %get-tuple-element.81), kind=kOutput, calls=%fused_computation.28 | convolution fusion | flops 76972032 | bytes 3538944 | tf_op jit(solution)/shard_map/nthe,nhde->nthd/dot_general | solution.py:113
  54.7 2.4 %copy.65 = bf16[3,128,6,128]{3,2,1,0:T(8,128)(2,1)} copy(bf16[3,128,6,128]{1,3,2,0:T(8,128)(2,1)} %fusion.15) | data formatting | bytes 1179648 | tf_op jit(solution)/shard_map/mul | solution.py:111
  57.0 2.5 %stack.12 = bf16[1,1,384,768]{3,2,1,0:T(8,128)(2,1)} reshape(bf16[3,128,6,128]{3,2,1,0:T(8,128)(2,1)} %copy.65) | data formatting | bytes 1179648 | tf_op jit(solution)/shard_map/stack | solution.py:124
  59.5 1.4 %pad_maximum_fusion = bf16[1,3,384,768]{3,2,1,0:T(8,128)(2,1)S(1)} fusion(bf16[1,1,384,768]{3,2,1,0:T(8,128)(2,1)} %stack.14, bf16[1,1,384,768]{3,2,1,0:T(8,128)(2,1)S(1)} %copy-done.10, bf16[1,1,384,768]{3,2,1,0:T(8,128)(2,1)} %stack.12), kind=kLoop, calls=%fused_computation.2 | loop fusion | flops 1769472 | bytes 3538944 | tf_op jit(solution)/shard_map/stack | solution.py:124
  61.0 3.6 %collective-permute-start = (bf16[1,3,384,768]{3,2,1,0:T(8,128)(2,1)S(1)}, bf16[1,3,384,768]{3,2,1,0:T(8,128)(2,1)S(1)}, u32[]{:S(2)}, u32[]{:S(2)}) collective-permute-start(bf16[1,3,384,768]{3,2,1,0:T(8,128)(2,1)S(1)} %pad_maximum_fusion), channel_id=1, source_target_pairs={{0,12},{4,0},{8,4},{12,8},{1,13},{5,1},{9,5},{13,9},{2,14},{6,2},{... | collective-permute-start | bytes 5308424 | tf_op jit(solution)/shard_map/ppermute | solution.py:27
  65.6 1.6 %collective-permute-start.1 = (f32[384]{0:T(512)S(1)}, f32[384]{0:T(512)S(1)}, u32[]{:S(2)}, u32[]{:S(2)}) collective-permute-start(f32[384]{0:T(512)S(1)} %bitcast.89), channel_id=1, source_target_pairs={{0,1},{1,0},{2,3},{3,2},{4,5},{5,4},{6,7},{7,6},{8,9},{9,8},{10,11... | collective-permute-start | bytes 4616 | tf_op jit(solution)/shard_map/ppermute | solution.py:108
  67.2 2.0 %collective-permute-done.1 = f32[384]{0:T(512)S(1)} collective-permute-done((f32[384]{0:T(512)S(1)}, f32[384]{0:T(512)S(1)}, u32[]{:S(2)}, u32[]{:S(2)}) %collective-permute-start.1) | collective-permute-done | bytes 1568 | tf_op jit(solution)/shard_map/ppermute | solution.py:108
  69.2 2.6 %collective-permute-start.2 = (f32[384]{0:T(512)S(1)}, f32[384]{0:T(512)S(1)}, u32[]{:S(2)}, u32[]{:S(2)}) collective-permute-start(f32[384]{0:T(512)S(1)} %bitcast_add_fusion.2), channel_id=1, source_target_pairs={{0,2},{1,3},{2,0},{3,1},{4,6},{5,7},{6,4},{7,5},{8,10},{9,11},{10,... | collective-permute-start | bytes 4616 | tf_op jit(solution)/shard_map/ppermute | solution.py:108
  71.8 1.9 %collective-permute-done.2 = f32[384]{0:T(512)S(1)} collective-permute-done((f32[384]{0:T(512)S(1)}, f32[384]{0:T(512)S(1)}, u32[]{:S(2)}, u32[]{:S(2)}) %collective-permute-start.2) | collective-permute-done | bytes 1568 | tf_op jit(solution)/shard_map/ppermute | solution.py:108
  74.3 27.6 %collective-permute-done = bf16[1,3,384,768]{3,2,1,0:T(8,128)(2,1)S(1)} collective-permute-done((bf16[1,3,384,768]{3,2,1,0:T(8,128)(2,1)S(1)}, bf16[1,3,384,768]{3,2,1,0:T(8,128)(2,1)S(1)}, u32[]{:S(2)}, u32[]{:S(2)}) %collective-permute-start) | collective-permute-done | bytes 1769504 | tf_op jit(solution)/shard_map/ppermute | solution.py:27
  101.9 1.2 %copy.113 = bf16[1,3,384,768]{3,2,1,0:T(8,128)(2,1)} copy(bf16[1,3,384,768]{3,2,1,0:T(8,128)(2,1)S(1)} %collective-permute-done) | data formatting | bytes 3538944
  (52 shorter events, 11.2 us)
Async XLA Ops:
  0.6 1.5 %copy-start = (bf16[1,512,768]{2,1,0:T(8,128)(2,1)S(1)}, bf16[1,512,768]{2,1,0:T(8,128)(2,1)}, u32[]{:S(2)}) copy-start(bf16[1,512,768]{2,1,0:T(8,128)(2,1)} %param.11) | copy-start | bytes 2359300
  5.9 15.9 %copy-start.1 = (bf16[3,128,768]{1,2,0:T(8,128)(2,1)}, bf16[3,128,768]{1,2,0:T(8,128)(2,1)S(1)}, u32[]{:S(2)}) copy-start(bf16[3,128,768]{1,2,0:T(8,128)(2,1)S(1)} %copy.56) | copy-start | bytes 1769476
  5.9 4.5 %copy-start.12 = (bf16[1,512,768]{2,1,0:T(8,128)(2,1)S(1)}, bf16[1,512,768]{2,1,0:T(8,128)(2,1)}, u32[]{:S(2)}) copy-start(bf16[1,512,768]{2,1,0:T(8,128)(2,1)} %param.14) | copy-start | bytes 2359300
  12.3 2.5 %copy-start.13 = (f32[1,512]{1,0:T(1,128)S(1)}, f32[1,512]{1,0:T(1,128)}, u32[]{:S(2)}) copy-start(f32[1,512]{1,0:T(1,128)} %param.15) | copy-start | bytes 6148
  16.4 1.3 %copy-start.3 = (f32[3,128,768]{1,2,0:T(8,128)S(1)}, f32[3,128,768]{1,2,0:T(8,128)}, u32[]{:S(2)}) copy-start(f32[3,128,768]{1,2,0:T(8,128)} %copy.58) | copy-start | bytes 3538948
  27.4 1.1 %copy-start.11 = (f32[6,128,128]{2,1,0:T(8,128)S(1)}, f32[6,128,128]{2,1,0:T(8,128)}, u32[]{:S(2)}) copy-start(f32[6,128,128]{2,1,0:T(8,128)} %get-tuple-element.99) | copy-start | bytes 1179652
  37.4 1.5 %copy-start.9 = (f32[3,6,128,128]{3,2,1,0:T(8,128)S(1)}, f32[3,6,128,128]{3,2,1,0:T(8,128)}, u32[]{:S(2)}) copy-start(f32[3,6,128,128]{3,2,1,0:T(8,128)} %fusion.33) | copy-start | bytes 3538948
  37.5 0.8 copy-start.7
  40.0 4.8 %copy-start.6 = (bf16[3,6,128,128]{3,2,1,0:T(8,128)(2,1)S(1)}, bf16[3,6,128,128]{3,2,1,0:T(8,128)(2,1)}, u32[]{:S(2)}) copy-start(bf16[3,6,128,128]{3,2,1,0:T(8,128)(2,1)} %fusion.10) | copy-start | bytes 1769476
  44.8 1.1 %copy-start.2 = (bf16[3,128,768]{1,2,0:T(8,128)(2,1)S(1)}, bf16[3,128,768]{1,2,0:T(8,128)(2,1)}, u32[]{:S(2)}) copy-start(bf16[3,128,768]{1,2,0:T(8,128)(2,1)} %copy-done.1) | copy-start | bytes 1769476
  44.8 1.2 %copy-start.8 = (bf16[3,6,128,128]{3,2,1,0:T(8,128)(2,1)S(1)}, bf16[3,6,128,128]{3,2,1,0:T(8,128)(2,1)}, u32[]{:S(2)}) copy-start(bf16[3,6,128,128]{3,2,1,0:T(8,128)(2,1)} %copy-done.7) | copy-start | bytes 1769476
  54.7 4.8 %copy-start.10 = (bf16[1,1,384,768]{3,2,1,0:T(8,128)(2,1)S(1)}, bf16[1,1,384,768]{3,2,1,0:T(8,128)(2,1)}, u32[]{:S(2)}) copy-start(bf16[1,1,384,768]{3,2,1,0:T(8,128)(2,1)} %stack.13) | copy-start | bytes 1769476
  60.9 4.2 %copy-start.4 = (f32[3,128,768]{1,2,0:T(8,128)S(1)}, f32[3,128,768]{1,2,0:T(8,128)}, u32[]{:S(2)}) copy-start(f32[3,128,768]{1,2,0:T(8,128)} %copy.58) | copy-start | bytes 3538948
  61.0 4.2 %copy-start.5 = (f32[2,6,128,128]{3,2,1,0:T(8,128)S(1)}, f32[2,6,128,128]{3,2,1,0:T(8,128)}, u32[]{:S(2)}) copy-start(f32[2,6,128,128]{3,2,1,0:T(8,128)} %slice.8) | copy-start | bytes 2359300
  61.0 40.9 %collective-permute-start = (bf16[1,3,384,768]{3,2,1,0:T(8,128)(2,1)S(1)}, bf16[1,3,384,768]{3,2,1,0:T(8,128)(2,1)S(1)}, u32[]{:S(2)}, u32[]{:S(2)}) collective-permute-start(bf16[1,3,384,768]{3,2,1,0:T(8,128)(2,1)S(1)} %pad_maximum_fusion), channel_id=1, source_target_pairs={{0,12},{4,0},{8,4},{12,8},{1,13},{5,1},{9,5},{13,9},{2,14},{6,2},{... | collective-permute-start | bytes 5308424 | tf_op jit(solution)/shard_map/ppermute | solution.py:27
  65.6 3.6 %collective-permute-start.1 = (f32[384]{0:T(512)S(1)}, f32[384]{0:T(512)S(1)}, u32[]{:S(2)}, u32[]{:S(2)}) collective-permute-start(f32[384]{0:T(512)S(1)} %bitcast.89), channel_id=1, source_target_pairs={{0,1},{1,0},{2,3},{3,2},{4,5},{5,4},{6,7},{7,6},{8,9},{9,8},{10,11... | collective-permute-start | bytes 4616 | tf_op jit(solution)/shard_map/ppermute | solution.py:108
  69.2 4.5 %collective-permute-start.2 = (f32[384]{0:T(512)S(1)}, f32[384]{0:T(512)S(1)}, u32[]{:S(2)}, u32[]{:S(2)}) collective-permute-start(f32[384]{0:T(512)S(1)} %bitcast_add_fusion.2), channel_id=1, source_target_pairs={{0,2},{1,3},{2,0},{3,1},{4,6},{5,7},{6,4},{7,5},{8,10},{9,11},{10,... | collective-permute-start | bytes 4616 | tf_op jit(solution)/shard_map/ppermute | solution.py:108
